TPU v7x, 128 devices: a whole 4x4x4 slice. The times are simulated.
128 devices in a mesh: group: 4 (over y), ctx: 32 (over x, z, core).
Axes of the slice: x: 4, y: 4, z: 4, core: 2. Of those that a mesh axis runs over, the one named last changes fastest.
Arguments:
- query: bfloat16 [128, 128, 576], P('group', 'ctx'), may hold values from -160 to 160
- cache: bfloat16 [32, 32768, 576], P('group', 'ctx'), may hold values from -6 to 6
- new_keys: bfloat16 [128, 576], P('group'), may hold values from -7 to 7
- lengths: int32 [32], P('group'), may hold values from 1 to 32768, as said below
- value_up_weight: bfloat16 [128, 512, 128], P('ctx'), may hold values from -1 to 1
- w_out: bfloat16 [16384, 7168], P('ctx'), may hold values from -0.1875 to 0.1875
- residual: bfloat16 [128, 7168], P(('group', 'ctx')), may hold values from -6 to 6
- norm_gain: float32 [7168], replicated, may hold values from 0.1 to 1.9
- w_router: bfloat16 [7168, 16], replicated, may hold values from -0.125 to 0.125
- routes: int32 [128, 8], P(('group', 'ctx')), may hold values from 0 to 15, all different within a row
- w_gate: bfloat16 [7168, 32768], P(None, ('group', 'ctx')), may hold values from -0.0625 to 0.0625
- w_up: bfloat16 [7168, 32768], P(None, ('group', 'ctx')), may hold values from -0.0625 to 0.0625
- w_down: bfloat16 [32768, 7168], P(('group', 'ctx')), may hold values from -0.125 to 0.125
Outputs:
- attn_out: bfloat16 [128, 7168], P(('group', 'ctx'))
- layer_out: bfloat16 [128, 7168], P(('group', 'ctx'))
Inputs may be any that keep to these rules, and one draw needn't show every extreme that they name: `lengths`: some request has all 32768 positions live.
All inputs are finite; a program needn't handle non-finite values.
Results may differ from a plain program's by a relative error of at most 0.018.
Values may be sent and summed in bfloat16 or wider, within the bound.
No kernel may reach another device: no remote copies, remote signals or barrier semaphores. Data moves between devices by JAX's collectives and lax.ppermute only.
A program may use at most 192 MiB of HBM per device.

v0:
```python
import jax
import jax.numpy as jnp
from jax import lax
from jax.sharding import PartitionSpec as P

LATENT_WIDTH = 512
ROTARY_WIDTH = 64
QK_NOPE = 128
VALUE_HEAD_WIDTH = 128
EXPERTS = 16
neg_floor = -1e30
route_scale = 2.5
norm_eps = 1e-06


def expert_partial(slot_rows, w_gate, w_up, w_down):
    gate_sum = jnp.dot(slot_rows, w_gate, preferred_element_type=jnp.float32)
    up_sum = jnp.dot(slot_rows, w_up, preferred_element_type=jnp.float32)
    hidden = (jax.nn.silu(gate_sum) * up_sum).astype(jnp.bfloat16)
    return jnp.dot(hidden, w_down, preferred_element_type=jnp.float32)


def local(
    query,
    cache,
    new_keys,
    lengths,
    value_up_weight,
    w_out,
    residual,
    norm_gain,
    w_router,
    routes,
    w_gate,
    w_up,
    w_down,
):
    score_scale = (QK_NOPE + ROTARY_WIDTH) ** (-0.5)
    ctx_count = lax.axis_size("ctx")
    group_count = lax.axis_size("group")
    ctx_index = lax.axis_index("ctx")
    grouped_rows, local_heads, features = query.shape
    request_batch = lengths.shape[0]
    draft_tokens = grouped_rows // request_batch
    block_len = cache.shape[1]
    positions = ctx_index * block_len + jnp.arange(block_len, dtype=jnp.int32)
    live_mask = (positions[None, :] < lengths[:, None])[:, None, None, :]
    compressed_keys = cache[:, :, :LATENT_WIDTH]
    all_heads = lax.all_gather(query, "ctx", axis=1, tiled=True)
    current_width = all_heads.shape[1]
    shaped = all_heads.reshape(request_batch, draft_tokens, current_width, features)
    scores = score_scale * jnp.einsum(
        "rqhd,rtd->rqht", shaped, cache, preferred_element_type=jnp.float32
    )
    block_max = jnp.max(jnp.where(live_mask, scores, neg_floor), axis=-1)
    probability = jnp.exp(jnp.where(live_mask, scores - block_max[..., None], neg_floor))
    block_sum = jnp.sum(probability, axis=-1)
    block_result = jnp.einsum(
        "rqht,rtk->rqhk",
        probability.astype(jnp.bfloat16),
        compressed_keys,
        preferred_element_type=jnp.float32,
    )
    arrived = (
        lax.all_to_all(
            block_max.reshape(grouped_rows, current_width)[None],
            "ctx",
            split_axis=2,
            concat_axis=0,
            tiled=True,
        ),
        lax.all_to_all(
            block_sum.reshape(grouped_rows, current_width)[None],
            "ctx",
            split_axis=2,
            concat_axis=0,
            tiled=True,
        ),
        lax.all_to_all(
            block_result.reshape(grouped_rows, current_width, LATENT_WIDTH)[None],
            "ctx",
            split_axis=2,
            concat_axis=0,
            tiled=True,
        ),
    )
    cache_max = jnp.max(arrived[0], axis=0)
    factors = jnp.exp(arrived[0] - cache_max[None])
    cache_sum = jnp.sum(factors * arrived[1], axis=0)
    cache_result = jnp.sum(factors[..., None] * arrived[2], axis=0)
    own_query = query.reshape(request_batch, draft_tokens, local_heads, features)
    recent_keys = new_keys.reshape(request_batch, draft_tokens, features)
    near_scores = score_scale * jnp.einsum(
        "rqhd,rjd->rqhj", own_query, recent_keys, preferred_element_type=jnp.float32
    )
    causal = (
        jnp.arange(draft_tokens, dtype=jnp.int32)[None, :]
        <= jnp.arange(draft_tokens, dtype=jnp.int32)[:, None]
    )
    causal = causal[None, :, None, :]
    near_max = jnp.max(jnp.where(causal, near_scores, neg_floor), axis=-1)
    shaped_max = cache_max.reshape(request_batch, draft_tokens, local_heads)
    joint_max = jnp.maximum(shaped_max, near_max)
    cache_rescale = jnp.exp(shaped_max - joint_max)
    nearby_probability = jnp.exp(jnp.where(causal, near_scores - joint_max[..., None], neg_floor))
    denominator = cache_sum.reshape(
        request_batch, draft_tokens, local_heads
    ) * cache_rescale + jnp.sum(nearby_probability, axis=-1)
    softmax_numerator = cache_result.reshape(
        request_batch, draft_tokens, local_heads, LATENT_WIDTH
    ) * cache_rescale[..., None] + jnp.einsum(
        "rqhj,rjk->rqhk",
        nearby_probability,
        recent_keys[:, :, :LATENT_WIDTH].astype(jnp.float32),
        precision=lax.Precision.HIGHEST,
    )
    latent_vector = (
        (softmax_numerator / denominator[..., None])
        .astype(jnp.bfloat16)
        .reshape(grouped_rows, local_heads, LATENT_WIDTH)
    )
    per_head_values = jnp.einsum(
        "gxj,xjs->gxs", latent_vector, value_up_weight, preferred_element_type=jnp.float32
    )
    per_head_values = per_head_values.astype(jnp.bfloat16).reshape(
        grouped_rows, local_heads * VALUE_HEAD_WIDTH
    )
    row_count = residual.shape[0]
    attention = lax.psum_scatter(
        jnp.dot(per_head_values, w_out, preferred_element_type=jnp.float32).astype(jnp.bfloat16),
        "ctx",
        scatter_dimension=0,
        tiled=True,
    ).astype(jnp.float32)
    attn_out = attention.astype(jnp.bfloat16)
    stream = (residual.astype(jnp.float32) + attention).astype(jnp.bfloat16)
    stream_wide = stream.astype(jnp.float32)
    mean_square = jnp.mean(stream_wide * stream_wide, axis=-1, keepdims=True)
    normed = (stream_wide * lax.rsqrt(mean_square + norm_eps) * norm_gain).astype(jnp.bfloat16)
    gate_values = jax.nn.sigmoid(jnp.dot(normed, w_router, preferred_element_type=jnp.float32))
    expert_ids = jnp.arange(EXPERTS, dtype=jnp.int32)
    selected_experts = (routes[:, :, None] == expert_ids[None, None, :]).astype(jnp.float32)
    picked = jnp.sum(selected_experts * gate_values[:, None, :], axis=-1)
    route_weights = route_scale * picked / jnp.sum(picked, axis=-1, keepdims=True)
    device_count = group_count * ctx_count
    slices = device_count // EXPERTS
    owners = jnp.arange(device_count, dtype=jnp.int32) // slices
    row_ids = jnp.arange(row_count, dtype=jnp.int32)
    earlier = row_ids[:, None] > row_ids[None, :]
    same_expert = routes[:, :, None, None] == routes[None, None, :, :]
    slot_index = jnp.sum((same_expert & earlier[:, None, :, None]).astype(jnp.int32), axis=(2, 3))
    targets = (routes[:, :, None] == owners[None, None, :])[..., None] & (
        slot_index[:, :, None, None] == row_ids[None, None, None, :]
    )
    placing = jnp.sum(targets.astype(jnp.float32), axis=1)
    coefficient = jnp.sum(route_weights[:, :, None, None] * targets.astype(jnp.float32), axis=1)
    outgoing = jnp.einsum(
        "idc,ij->dcj", placing.astype(jnp.bfloat16), normed, preferred_element_type=jnp.float32
    ).astype(jnp.bfloat16)
    model_width = residual.shape[1]
    slot_block = lax.all_to_all(outgoing, ("group", "ctx"), split_axis=0, concat_axis=0, tiled=True)
    slot_span = slot_block.shape[1]
    partial_out = expert_partial(
        slot_block.reshape(device_count * slot_span, model_width), w_gate, w_up, w_down
    )
    returned = lax.all_to_all(
        partial_out.reshape(device_count, slot_span, model_width).astype(jnp.bfloat16),
        ("group", "ctx"),
        split_axis=0,
        concat_axis=0,
        tiled=True,
    ).astype(jnp.float32)
    expert_mix = jnp.einsum("idc,dcj->ij", coefficient, returned, precision=lax.Precision.HIGHEST)
    layer_out = (stream_wide + expert_mix).astype(jnp.bfloat16)
    return (attn_out, layer_out)


def solution(mesh):
    return jax.shard_map(
        local,
        mesh=mesh,
        in_specs=(
            P("group", "ctx", None),
            P("group", "ctx", None),
            P("group", None),
            P("group"),
            P("ctx", None, None),
            P("ctx", None),
            P(("group", "ctx"), None),
            P(),
            P(),
            P(("group", "ctx"), None),
            P(None, ("group", "ctx")),
            P(None, ("group", "ctx")),
            P(("group", "ctx"), None),
        ),
        out_specs=(P(("group", "ctx"), None), P(("group", "ctx"), None)),
        check_vma=False,
    )
```

profile of v0, /device:TPU:1, one launch (start us, length us, event | category | flops | bytes accessed | tf_op | source)
XLA Modules:
  0.0 506.6 jit_solution(4167287995145306483)
XLA Ops:
  7.2 0.0 copy-start
  7.2 0.0 all-gather.2.cloned.1.call-start
  7.2 1.6 copy.86
  8.9 0.0 all-gather.2.cloned.1.call-update
  8.9 0.7 broadcast_compare_fusion
  9.6 51.8 %all-gather.2.cloned.1.call-done = bf16[32,128,576]{2,0,1:T(8,128)(2,1)} async-done(((bf16[32,4,576]{2,0,1:T(8,128)(2,1)}), bf16[32,128,576]{2,0,1:T(8,128)(2,1)}) %all-gather.2.cloned.1.call-update) | async-done | bytes 4718608 | tf_op jit(solution)/shard_map/all_gather | solution.py:49
  61.5 8.7 %copy.87 = bf16[32,128,576]{1,2,0:T(8,128)(2,1)} copy(bf16[32,128,576]{2,0,1:T(8,128)(2,1)} %all-gather.2.cloned.1.call-done) | data formatting | bytes 9437184 | tf_op jit(solution)/shard_map/all_gather | solution.py:49
  70.1 10.9 %select_reduce_fusion = (f32[8,4,128]{2,1,0:T(4,128)S(1)}, f32[8,4,128,1024]{3,2,1,0:T(8,128)S(1)}) fusion(pred[8,1024]{1,0:T(8,128)(4,1)S(1)} %broadcast_compare_fusion, bf16[8,4,128,576]{2,3,1,0:T(8,128)(2,1)} %bitcast.110, bf16[8,1024,576]{1,2,0:T(8,128)(2,1)} %param.14), kind=kOutput, calls=%fused_computation.1 | convolution fusion | flops 4844417024 | bytes 30957568 | tf_op jit(solution)/shard_map/rqhd,rtd->rqht/dot_general | solution.py:52
  81.1 4.4 fusion
  85.5 1.3 copy-done.1
  86.8 0.1 copy.95
  86.9 0.5 broadcast.318
  87.4 0.8 reduce.9
  88.2 0.7 reshape.421
  88.9 5.3 %all-to-all-start.2 = ((f32[32,1,128]{2,1,0:T(1,128)}), f32[32,1,128]{2,1,0:T(1,128)S(1)}, u32[]{:S(2)}, u32[]{:S(2)}) async-start(f32[32,1,128]{2,1,0:T(1,128)} %reshape.421), calls=%async_computation.2 | async-start | bytes 32768 | tf_op jit(solution)/shard_map/all_to_all | solution.py:72
  94.2 0.1 copy.88
  94.3 0.8 reduce.11
  95.1 0.7 reshape.419
  95.8 5.3 %all-to-all-done.2 = f32[32,1,128]{2,1,0:T(1,128)S(1)} async-done(((f32[32,1,128]{2,1,0:T(1,128)}), f32[32,1,128]{2,1,0:T(1,128)S(1)}, u32[]{:S(2)}, u32[]{:S(2)}) %all-to-all-start.2) | async-done | bytes 16416 | tf_op jit(solution)/shard_map/all_to_all | solution.py:72
  101.1 4.1 all-to-all-start
  105.2 13.0 %fusion.4 = f32[8,4,128,512]{3,2,1,0:T(8,128)} fusion(f32[8,4,128,1024]{3,2,1,0:T(8,128)} %copy-done.1, bf16[8,1024,576]{1,2,0:T(8,128)(2,1)} %param.14, f32[8,4,128]{2,1,0:T(4,128)S(1)} %get-tuple-element.13, pred[8,1024]{1,0:T(8,128)(4,1)S(1)} %broadcast_compare_fusion), kind=kOutput, calls=%fused_computation.7 | convolution fusion | flops 4311744512 | bytes 33579008 | tf_op jit(solution)/shard_map/rqht,rtk->rqhk/dot_general | solution.py:58
  118.2 11.5 %copy.90 = f32[1,32,128,512]{3,1,0,2:T(8,128)} copy(f32[1,32,128,512]{3,2,1,0:T(8,128)} %bitcast.109) | data formatting | bytes 16777216 | tf_op jit(solution)/shard_map/broadcast_in_dim;reshape | solution.py:80
  129.7 7.7 %all-to-all-start.1 = ((f32[1,32,128,512]{3,1,0,2:T(8,128)}), f32[1,32,128,512]{3,1,0,2:T(8,128)}, u32[]{:S(2)}, u32[]{:S(2)}) async-start(f32[1,32,128,512]{3,1,0,2:T(8,128)} %copy.90), calls=%async_computation.1 | async-start | bytes 16777216 | tf_op jit(solution)/shard_map/all_to_all | solution.py:79
  137.4 0.3 all-reduce.3.cloned.1.call-start
  137.7 1.0 select_reduce_fusion.1
  138.7 0.7 reduce.10
  139.4 0.1 reshape.422
  139.6 0.7 reduce.12
  140.2 0.1 reshape.420
  140.4 0.1 copy.107
  140.5 0.1 multiply_reduce_fusion.1
  140.6 0.1 copy.106
  140.7 0.1 fusion.45
  140.8 105.1 %all-to-all-done.1 = f32[1,32,128,512]{3,1,0,2:T(8,128)} async-done(((f32[1,32,128,512]{3,1,0,2:T(8,128)}), f32[1,32,128,512]{3,1,0,2:T(8,128)}, u32[]{:S(2)}, u32[]{:S(2)}) %all-to-all-start.1) | async-done | bytes 8388640 | tf_op jit(solution)/shard_map/all_to_all | solution.py:79
  245.9 3.8 multiply_reduce_fusion
  249.8 0.2 copy.91
  250.0 0.5 fusion.22
  250.5 0.2 fusion.29
  250.7 0.0 copy-start.8
  250.7 0.0 copy-start.7
  250.8 0.0 copy-start.6
  250.8 5.3 %convolution_convert_fusion.1 = bf16[32,7168]{1,0:T(8,128)(2,1)} fusion(bf16[512,7168]{1,0:T(8,128)(2,1)} %param.18, bf16[4,4,8,128]{3,2,1,0:T(8,128)(2,1)S(1)} %fusion.29), kind=kOutput, calls=%fused_computation.16 | convolution fusion | flops 235110400 | bytes 7831552 | tf_op jit(solution)/shard_map/dot_general | solution.py:130
  256.1 0.0 all-reduce.3.cloned.1.call-update
  256.1 0.6 dynamic-slice
  256.7 117.4 %all-reduce.3.cloned.1.call-done = bf16[32,7168]{1,0:T(8,128)(2,1)} async-done(((bf16[32,7168]{1,0:T(8,128)(2,1)}), bf16[32,7168]{1,0:T(8,128)(2,1)}) %all-reduce.3.cloned.1.call-update) | async-done | bytes 458768
  374.1 2.8 multiply_reduce_fusion.2
  377.6 0.1 convert_reduce_fusion
  377.7 0.2 fusion.33
  377.9 0.7 select_reduce_fusion.2
  378.6 0.6 multiply_divide_fusion
  379.3 0.1 fusion.54
  379.4 0.3 fusion.14
  379.7 0.5 broadcast.322
  380.2 2.7 reduce.13
  382.9 4.6 reshape.423
  387.5 35.5 %all_to_all.64 = bf16[128,2,3584]{2,1,0:T(2,128)(2,1)} all-to-all(bf16[128,2,3584]{2,1,0:T(2,128)(2,1)S(1)} %reshape.423), channel_id=1, replica_groups=mesh['group'=4,'ctx'=32] {'group','ctx'}, dimensions={0} | all-to-all | bytes 3670016 | tf_op jit(solution)/shard_map/all_to_all | solution.py:161
  423.0 11.5 %reshape.424 = bf16[128,1,7168]{2,1,0:T(2,128)(2,1)} reshape(bf16[128,2,3584]{2,1,0:T(2,128)(2,1)} %all_to_all.64) | data formatting | bytes 3670016
  434.5 3.9 fusion.19
  438.5 6.3 %fusion.12 = bf16[128,1,7168]{2,0,1:T(8,128)(2,1)S(1)} fusion(bf16[256,7168]{1,0:T(8,128)(2,1)} %param.25, bf16[7168,256]{1,0:T(8,128)(2,1)} %param.24, bf16[128,1,7168]{2,1,0:T(2,128)(2,1)} %reshape.424, f32[128,256]{1,0:T(8,128)S(1)} %fusion.19), kind=kOutput, calls=%fused_computation.15 | convolution fusion | flops 940638208 | bytes 11141120 | tf_op jit(solution)/shard_map/dot_general | solution.py:20
  444.8 2.7 reduce.14
  447.5 4.6 reshape.425
  452.1 32.3 %all_to_all.65 = bf16[128,2,3584]{2,1,0:T(2,128)(2,1)} all-to-all(bf16[128,2,3584]{2,1,0:T(2,128)(2,1)S(1)} %reshape.425), channel_id=1, replica_groups=mesh['group'=4,'ctx'=32] {'group','ctx'}, dimensions={0} | all-to-all | bytes 3670016 | tf_op jit(solution)/shard_map/all_to_all | solution.py:166
  484.4 11.5 %reshape.426 = bf16[128,1,7168]{2,1,0:T(2,128)(2,1)} reshape(bf16[128,2,3584]{2,1,0:T(2,128)(2,1)} %all_to_all.65) | data formatting | bytes 3670016
  495.9 3.8 fusion.13
  (24 shorter events, 0.2 us)
Async XLA Ops:
  7.2 243.3 %copy-start = (bf16[4,512,128]{2,1,0:T(8,128)(2,1)S(1)}, bf16[4,512,128]{2,1,0:T(8,128)(2,1)}, u32[]{:S(2)}) copy-start(bf16[4,512,128]{2,1,0:T(8,128)(2,1)} %param.17) | copy-start | bytes 1572868
  7.2 54.3 %all-gather.2.cloned.1.call-start = ((), (), s32[]{:S(2)}) async-start(), calls=%async_computation.5 | async-start | bytes 5406720 | tf_op jit(solution)/shard_map/all_gather | solution.py:49
  81.1 5.7 %copy-start.1 = (f32[8,4,128,1024]{3,2,1,0:T(8,128)}, f32[8,4,128,1024]{3,2,1,0:T(8,128)S(1)}, u32[]{:S(2)}) copy-start(f32[8,4,128,1024]{3,2,1,0:T(8,128)S(1)} %get-tuple-element.14) | copy-start | bytes 50331652
  88.9 12.1 %all-to-all-start.2 = ((f32[32,1,128]{2,1,0:T(1,128)}), f32[32,1,128]{2,1,0:T(1,128)S(1)}, u32[]{:S(2)}, u32[]{:S(2)}) async-start(f32[32,1,128]{2,1,0:T(1,128)} %reshape.421), calls=%async_computation.2 | async-start | bytes 32768 | tf_op jit(solution)/shard_map/all_to_all | solution.py:72
  101.1 28.6 %all-to-all-start = ((f32[32,1,128]{2,1,0:T(1,128)}), f32[32,1,128]{2,1,0:T(1,128)S(1)}, u32[]{:S(2)}, u32[]{:S(2)}) async-start(f32[32,1,128]{2,1,0:T(1,128)} %reshape.419), calls=%async_computation | async-start | bytes 32768 | tf_op jit(solution)/shard_map/all_to_all | solution.py:65
  129.7 8.0 %copy-start.3 = (bf16[32,576]{1,0:T(8,128)(2,1)S(1)}, bf16[32,576]{1,0:T(8,128)(2,1)}, u32[]{:S(2)}) copy-start(bf16[32,576]{1,0:T(8,128)(2,1)} %param.15) | copy-start | bytes 110596
  129.7 8.0 %copy-start.2 = (bf16[32,4,576]{2,1,0:T(4,128)(2,1)S(1)}, bf16[32,4,576]{2,1,0:T(4,128)(2,1)}, u32[]{:S(2)}) copy-start(bf16[32,4,576]{2,1,0:T(4,128)(2,1)} %param.13) | copy-start | bytes 442372
  129.7 116.2 %all-to-all-start.1 = ((f32[1,32,128,512]{3,1,0,2:T(8,128)}), f32[1,32,128,512]{3,1,0,2:T(8,128)}, u32[]{:S(2)}, u32[]{:S(2)}) async-start(f32[1,32,128,512]{3,1,0,2:T(8,128)} %copy.90), calls=%async_computation.1 | async-start | bytes 16777216 | tf_op jit(solution)/shard_map/all_to_all | solution.py:79
  137.4 236.7 %all-reduce.3.cloned.1.call-start = ((), (), s32[]{:S(2)}) async-start(), calls=%async_computation.6 | async-start | bytes 917504
  250.7 5.4 %copy-start.8 = (u32[128]{0:T(128)S(1)}, u32[128]{0:T(128)}, u32[]{:S(2)}) copy-start(u32[128]{0:T(128)} %constant.59) | copy-start | bytes 1540
  250.7 123.4 %copy-start.4 = (bf16[1,7168]{1,0:T(2,128)(2,1)S(1)}, bf16[1,7168]{1,0:T(2,128)(2,1)}, u32[]{:S(2)}) copy-start(bf16[1,7168]{1,0:T(2,128)(2,1)} %param.19) | copy-start | bytes 43012
  250.7 126.9 %copy-start.5 = (f32[7168]{0:T(1024)S(1)}, f32[7168]{0:T(1024)}, u32[]{:S(2)}) copy-start(f32[7168]{0:T(1024)} %param.20) | copy-start | bytes 86020
  250.7 127.0 %copy-start.7 = (bf16[7168,16]{0,1:T(8,128)(2,1)S(1)}, bf16[7168,16]{0,1:T(8,128)(2,1)}, u32[]{:S(2)}) copy-start(bf16[7168,16]{0,1:T(8,128)(2,1)} %param.21) | copy-start | bytes 688132
  250.8 127.2 %copy-start.6 = (s32[1,8]{1,0:T(1,128)S(1)}, s32[1,8]{1,0:T(1,128)}, u32[]{:S(2)}) copy-start(s32[1,8]{1,0:T(1,128)} %param.22) | copy-start | bytes 100
Sparse Core Ops, SparseCore 0:
  10.3 51.1 all-gather.1
  256.2 117.8 all-reduce.2
where the time goes:
time: 508 us; the launch traced here: 507 us
  waiting for transfers between devices  280 us (55%)
  blocking collectives  67.9 us (13%)
  local copies, waits for them, and re-layouts  59.1 us (12%)
  matrix products  45.3 us (9%)
  other arithmetic  22.2 us (4%)
  starting transfers between devices  17.4 us (3%)
  between operations  15.1 us (3%)
    unnamed x3, waiting for transfers between devices  117 us
    all_to_all x1, waiting for transfers between devices, local(): lax.all_to_all(block_result.reshape(grouped_rows, current_width, LATENT_W...  105 us
    all_gather x1, waiting for transfers between devices, local(): all_heads = lax.all_gather(query, 'ctx', axis=1, tiled=True)  51.8 us
    unnamed x29, local copies, waits for them, and re-layouts  37.8 us
    all_to_all x1, blocking collectives, local(): lax.all_to_all(outgoing, ('group', 'ctx'), split_axis=0, concat_axis=0, t...  35.5 us
    all_to_all x1, blocking collectives, local(): lax.all_to_all(partial_out.reshape(device_count, slot_span, model_width)....  32.3 us
    dot_general x1, matrix products, local(): jnp.einsum('rqht,rtk->rqhk', probability.astype(jnp.bfloat16), compressed...  13 us
    another operation x1, local copies, waits for them, and re-layouts, local(): block_result.reshape(grouped_rows, current_width, LATENT_WIDTH)[None]  11.5 us
  transfers between devices with their start and end apart: 5, of which 4 were waited for; matrix products, arithmetic and copies ran while one was open for 6% of the time, Pallas kernels for 0%

commit v1 on v0

--- a/solution.py
+++ b/solution.py
@@ -11,6 +11,11 @@
 neg_floor = -1e30
 route_scale = 2.5
 norm_eps = 1e-06
+
+
+def exchange_gather(x, axis, along):
+    outgoing = jnp.stack([x] * lax.axis_size(axis))
+    return jnp.concatenate(lax.all_to_all(outgoing, axis, 0, 0), axis=along)
 
 
 def expert_partial(slot_rows, w_gate, w_up, w_down):
@@ -46,7 +51,7 @@
     positions = ctx_index * block_len + jnp.arange(block_len, dtype=jnp.int32)
     live_mask = (positions[None, :] < lengths[:, None])[:, None, None, :]
     compressed_keys = cache[:, :, :LATENT_WIDTH]
-    all_heads = lax.all_gather(query, "ctx", axis=1, tiled=True)
+    all_heads = exchange_gather(query, "ctx", 1)
     current_width = all_heads.shape[1]
     shaped = all_heads.reshape(request_batch, draft_tokens, current_width, features)
     scores = score_scale * jnp.einsum(

time: 508 us -> 546 us (1.075)
  starting transfers between devices: 17.4 us -> 31.5 us
  waiting for transfers between devices: 280 us -> 292 us
  local copies, waits for them, and re-layouts: 59.1 us -> 71.1 us
    all_to_all x0 -> x1, waiting for transfers between devices: none -> 64.5 us  [exchange_gather(): return jnp.concatenate(lax.all_to_all(outgoing, axis, 0, 0), axis=along)]
    all_gather x1 -> x0, waiting for transfers between devices: 51.8 us -> none  [local(): all_heads = lax.all_gather(query, 'ctx', axis=1, tiled=True)]
    another operation x0 -> x2, local copies, waits for them, and re-layouts: none -> 14.8 us  [the longest x1 9.11 us: local(): all_heads.reshape(request_batch, draft_tokens, current_width, features)]
    all_to_all x0 -> x1, starting transfers between devices: none -> 9.61 us  [exchange_gather(): return jnp.concatenate(lax.all_to_all(outgoing, axis, 0, 0), axis=along)]
    all_gather x1 -> x0, local copies, waits for them, and re-layouts: 8.67 us -> none  [local(): all_heads = lax.all_gather(query, 'ctx', axis=1, tiled=True)]
    reshape x0 -> x1, local copies, waits for them, and re-layouts: none -> 7.56 us  [exchange_gather(): return jnp.concatenate(lax.all_to_all(outgoing, axis, 0, 0), axis=along)]
    unnamed x29 -> x30, local copies, waits for them, and re-layouts: 37.8 us -> 36.2 us
    unnamed x3 -> x2, waiting for transfers between devices: 117 us -> 118 us
  transfers between devices with their start and end apart: 5 -> 5, of which waited for: 4 -> 4; matrix products, arithmetic and copies ran while one was open for 6% -> 5% of each run, Pallas kernels for 0% -> 0%
where the time goes in v1:
time: 546 us; the launch traced here: 545 us
  waiting for transfers between devices  292 us (53%)
  local copies, waits for them, and re-layouts  71.1 us (13%)
  blocking collectives  67.9 us (12%)
  matrix products  45 us (8%)
  starting transfers between devices  31.5 us (6%)
  other arithmetic  21.6 us (4%)
  between operations  15.1 us (3%)
    unnamed x2, waiting for transfers between devices  118 us
    all_to_all x1, waiting for transfers between devices, local(): lax.all_to_all(block_result.reshape(grouped_rows, current_width, LATENT_W...  105 us
    all_to_all x1, waiting for transfers between devices, exchange_gather(): return jnp.concatenate(lax.all_to_all(outgoing, axis, 0, 0), axis=along)  64.5 us
    unnamed x30, local copies, waits for them, and re-layouts  36.2 us
    all_to_all x1, blocking collectives, local(): lax.all_to_all(outgoing, ('group', 'ctx'), split_axis=0, concat_axis=0, t...  35.5 us
    all_to_all x1, blocking collectives, local(): lax.all_to_all(partial_out.reshape(device_count, slot_span, model_width)....  32.3 us
    dot_general x1, matrix products, local(): jnp.einsum('rqht,rtk->rqhk', probability.astype(jnp.bfloat16), compressed...  13 us
    another operation x1, local copies, waits for them, and re-layouts, local(): block_result.reshape(grouped_rows, current_width, LATENT_WIDTH)[None]  11.5 us
  transfers between devices with their start and end apart: 5, of which 4 were waited for; matrix products, arithmetic and copies ran while one was open for 5% of the time, Pallas kernels for 0%

profile of v1, /device:TPU:1, one launch (start us, length us, event | category | flops | bytes accessed | tf_op | source)
XLA Modules:
  0.0 544.6 jit_solution(7461399432018236211)
XLA Ops:
  7.2 0.0 copy-start
  7.2 5.7 %stack.2 = bf16[32,32,4,576]{3,2,1,0:T(4,128)(2,1)} broadcast(bf16[32,4,576]{2,1,0:T(4,128)(2,1)} %param.13), dimensions={1,2,3} | broadcast | bytes 4866048 | tf_op jit(solution)/shard_map/stack | solution.py:17
  12.9 9.6 %all-to-all-start = ((bf16[32,32,4,576]{3,2,1,0:T(4,128)(2,1)}), bf16[32,32,4,576]{3,2,1,0:T(4,128)(2,1)}, u32[]{:S(2)}, u32[]{:S(2)}) async-start(bf16[32,32,4,576]{3,2,1,0:T(4,128)(2,1)} %stack.2), calls=%async_computation | async-start | bytes 10485760 | tf_op jit(solution)/shard_map/all_to_all | solution.py:18
  22.5 0.1 broadcast_compare_fusion
  22.6 64.5 %all-to-all-done = bf16[32,32,4,576]{3,2,1,0:T(4,128)(2,1)} async-done(((bf16[32,32,4,576]{3,2,1,0:T(4,128)(2,1)}), bf16[32,32,4,576]{3,2,1,0:T(4,128)(2,1)}, u32[]{:S(2)}, u32[]{:S(2)}) %all-to-all-start) | async-done | bytes 4718624 | tf_op jit(solution)/shard_map/all_to_all | solution.py:18
  87.1 7.6 %copy.86 = bf16[32,32,4,576]{3,2,1,0:T(4,128)(2,1)} copy(bf16[32,32,4,576]{3,2,0,1:T(4,128)(2,1)} %bitcast) | data formatting | bytes 9437184 | tf_op jit(solution)/shard_map/reshape | solution.py:18
  94.6 9.1 %reshape_reshape.3 = bf16[8,4,128,576]{3,2,1,0:T(8,128)(2,1)} reshape(bf16[32,32,4,576]{3,2,1,0:T(4,128)(2,1)} %copy.86) | data formatting | bytes 9437184 | tf_op jit(solution)/shard_map/reshape;reshape | solution.py:56
  103.7 10.7 %select_reduce_fusion = (f32[8,4,128]{2,1,0:T(4,128)S(1)}, f32[8,4,128,1024]{3,2,1,0:T(8,128)S(1)}) fusion(pred[8,1024]{1,0:T(8,128)(4,1)S(1)} %broadcast_compare_fusion, bf16[8,4,128,576]{3,2,1,0:T(8,128)(2,1)} %reshape_reshape.3, bf16[8,1024,576]{1,2,0:T(8,128)(2,1)} %param.14), kind=kOutput, calls=%fused_computation.1 | convolution fusion | flops 4844417024 | bytes 30957568 | tf_op jit(solution)/shard_map/rqhd,rtd->rqht/dot_general | solution.py:57
  114.4 4.4 fusion
  118.9 1.3 copy-done.1
  120.1 0.1 copy.95
  120.2 0.5 broadcast.320
  120.8 0.8 reduce.9
  121.6 0.7 reshape.423
  122.3 9.8 %all-to-all-start.3 = ((f32[32,1,128]{2,1,0:T(1,128)}), f32[32,1,128]{2,1,0:T(1,128)S(1)}, u32[]{:S(2)}, u32[]{:S(2)}) async-start(f32[32,1,128]{2,1,0:T(1,128)} %reshape.423), calls=%async_computation.3 | async-start | bytes 32768 | tf_op jit(solution)/shard_map/all_to_all | solution.py:77
  132.0 0.1 copy.88
  132.1 0.8 reduce.11
  132.9 0.7 reshape.421
  133.6 5.3 all-to-all-done.3
  138.9 4.1 all-to-all-start.1
  143.1 13.0 %fusion.4 = f32[8,4,128,512]{3,2,1,0:T(8,128)} fusion(f32[8,4,128,1024]{3,2,1,0:T(8,128)} %copy-done.1, bf16[8,1024,576]{1,2,0:T(8,128)(2,1)} %param.14, f32[8,4,128]{2,1,0:T(4,128)S(1)} %get-tuple-element.13, pred[8,1024]{1,0:T(8,128)(4,1)S(1)} %broadcast_compare_fusion), kind=kOutput, calls=%fused_computation.7 | convolution fusion | flops 4311744512 | bytes 33579008 | tf_op jit(solution)/shard_map/rqht,rtk->rqhk/dot_general | solution.py:63
  156.0 11.5 %copy.90 = f32[1,32,128,512]{3,1,0,2:T(8,128)} copy(f32[1,32,128,512]{3,2,1,0:T(8,128)} %bitcast.109) | data formatting | bytes 16777216 | tf_op jit(solution)/shard_map/broadcast_in_dim;reshape | solution.py:85
  167.5 7.7 %all-to-all-start.2 = ((f32[1,32,128,512]{3,1,0,2:T(8,128)}), f32[1,32,128,512]{3,1,0,2:T(8,128)}, u32[]{:S(2)}, u32[]{:S(2)}) async-start(f32[1,32,128,512]{3,1,0,2:T(8,128)} %copy.90), calls=%async_computation.2 | async-start | bytes 16777216 | tf_op jit(solution)/shard_map/all_to_all | solution.py:84
  175.2 0.3 all-reduce.3.cloned.1.call-start
  175.5 1.0 select_reduce_fusion.1
  176.5 0.7 reduce.10
  177.2 0.1 reshape.424
  177.4 0.7 reduce.12
  178.0 0.1 reshape.422
  178.2 0.1 copy.108
  178.3 0.1 multiply_reduce_fusion.1
  178.4 0.1 copy.107
  178.5 0.1 fusion.45
  178.6 105.1 %all-to-all-done.2 = f32[1,32,128,512]{3,1,0,2:T(8,128)} async-done(((f32[1,32,128,512]{3,1,0,2:T(8,128)}), f32[1,32,128,512]{3,1,0,2:T(8,128)}, u32[]{:S(2)}, u32[]{:S(2)}) %all-to-all-start.2) | async-done | bytes 8388640 | tf_op jit(solution)/shard_map/all_to_all | solution.py:84
  283.7 3.8 multiply_reduce_fusion
  287.6 0.2 copy.91
  287.8 0.5 fusion.22
  288.3 0.2 fusion.29
  288.5 0.0 copy-start.9
  288.5 0.0 copy-start.4
  288.6 0.0 copy-start.6
  288.6 5.3 convolution_convert_fusion.1
  293.9 0.0 all-reduce.3.cloned.1.call-update
  293.9 0.6 dynamic-slice
  294.5 117.6 %all-reduce.3.cloned.1.call-done = bf16[32,7168]{1,0:T(8,128)(2,1)} async-done(((bf16[32,7168]{1,0:T(8,128)(2,1)}), bf16[32,7168]{1,0:T(8,128)(2,1)}) %all-reduce.3.cloned.1.call-update) | async-done | bytes 458768
  412.1 2.8 multiply_reduce_fusion.2
  415.6 0.1 convert_reduce_fusion
  415.7 0.2 fusion.33
  415.9 0.7 select_reduce_fusion.2
  416.6 0.6 multiply_divide_fusion
  417.3 0.1 fusion.54
  417.4 0.3 fusion.14
  417.7 0.5 broadcast.324
  418.2 2.7 reduce.13
  420.9 4.6 reshape.425
  425.5 35.5 %all_to_all.69 = bf16[128,2,3584]{2,1,0:T(2,128)(2,1)} all-to-all(bf16[128,2,3584]{2,1,0:T(2,128)(2,1)S(1)} %reshape.425), channel_id=1, replica_groups=mesh['group'=4,'ctx'=32] {'group','ctx'}, dimensions={0} | all-to-all | bytes 3670016 | tf_op jit(solution)/shard_map/all_to_all | solution.py:166
  461.0 11.5 %reshape.426 = bf16[128,1,7168]{2,1,0:T(2,128)(2,1)} reshape(bf16[128,2,3584]{2,1,0:T(2,128)(2,1)} %all_to_all.69) | data formatting | bytes 3670016
  472.5 3.9 fusion.19
  476.5 6.3 %fusion.12 = bf16[128,1,7168]{2,0,1:T(8,128)(2,1)S(1)} fusion(bf16[256,7168]{1,0:T(8,128)(2,1)} %param.25, bf16[7168,256]{1,0:T(8,128)(2,1)} %param.24, bf16[128,1,7168]{2,1,0:T(2,128)(2,1)} %reshape.426, f32[128,256]{1,0:T(8,128)S(1)} %fusion.19), kind=kOutput, calls=%fused_computation.15 | convolution fusion | flops 940638208 | bytes 11141120 | tf_op jit(solution)/shard_map/dot_general | solution.py:25
  482.8 2.7 reduce.14
  485.5 4.6 reshape.427
  490.1 32.3 %all_to_all.70 = bf16[128,2,3584]{2,1,0:T(2,128)(2,1)} all-to-all(bf16[128,2,3584]{2,1,0:T(2,128)(2,1)S(1)} %reshape.427), channel_id=1, replica_groups=mesh['group'=4,'ctx'=32] {'group','ctx'}, dimensions={0} | all-to-all | bytes 3670016 | tf_op jit(solution)/shard_map/all_to_all | solution.py:171
  522.4 11.5 %reshape.428 = bf16[128,1,7168]{2,1,0:T(2,128)(2,1)} reshape(bf16[128,2,3584]{2,1,0:T(2,128)(2,1)} %all_to_all.70) | data formatting | bytes 3670016
  533.9 3.8 fusion.13
  (26 shorter events, 0.2 us)
Async XLA Ops:
  7.2 281.1 %copy-start = (bf16[4,512,128]{2,1,0:T(8,128)(2,1)S(1)}, bf16[4,512,128]{2,1,0:T(8,128)(2,1)}, u32[]{:S(2)}) copy-start(bf16[4,512,128]{2,1,0:T(8,128)(2,1)} %param.17) | copy-start | bytes 1572868
  12.9 9.6 %copy-start.7 = (s32[8]{0:T(128)S(1)}, s32[8]{0:T(128)}, u32[]{:S(2)}) copy-start(s32[8]{0:T(128)} %param.16) | copy-start | bytes 100
  12.9 74.2 %all-to-all-start = ((bf16[32,32,4,576]{3,2,1,0:T(4,128)(2,1)}), bf16[32,32,4,576]{3,2,1,0:T(4,128)(2,1)}, u32[]{:S(2)}, u32[]{:S(2)}) async-start(bf16[32,32,4,576]{3,2,1,0:T(4,128)(2,1)} %stack.2), calls=%async_computation | async-start | bytes 10485760 | tf_op jit(solution)/shard_map/all_to_all | solution.py:18
  114.4 5.7 %copy-start.1 = (f32[8,4,128,1024]{3,2,1,0:T(8,128)}, f32[8,4,128,1024]{3,2,1,0:T(8,128)S(1)}, u32[]{:S(2)}) copy-start(f32[8,4,128,1024]{3,2,1,0:T(8,128)S(1)} %get-tuple-element.14) | copy-start | bytes 50331652
  122.3 16.7 %all-to-all-start.3 = ((f32[32,1,128]{2,1,0:T(1,128)}), f32[32,1,128]{2,1,0:T(1,128)S(1)}, u32[]{:S(2)}, u32[]{:S(2)}) async-start(f32[32,1,128]{2,1,0:T(1,128)} %reshape.423), calls=%async_computation.3 | async-start | bytes 32768 | tf_op jit(solution)/shard_map/all_to_all | solution.py:77
  138.9 28.6 %all-to-all-start.1 = ((f32[32,1,128]{2,1,0:T(1,128)}), f32[32,1,128]{2,1,0:T(1,128)S(1)}, u32[]{:S(2)}, u32[]{:S(2)}) async-start(f32[32,1,128]{2,1,0:T(1,128)} %reshape.421), calls=%async_computation.1 | async-start | bytes 32768 | tf_op jit(solution)/shard_map/all_to_all | solution.py:70
  167.5 8.0 %copy-start.2 = (bf16[32,576]{1,0:T(8,128)(2,1)S(1)}, bf16[32,576]{1,0:T(8,128)(2,1)}, u32[]{:S(2)}) copy-start(bf16[32,576]{1,0:T(8,128)(2,1)} %param.15) | copy-start | bytes 110596
  167.5 8.1 %copy-start.3 = (bf16[32,4,576]{2,1,0:T(4,128)(2,1)S(1)}, bf16[32,4,576]{2,1,0:T(4,128)(2,1)}, u32[]{:S(2)}) copy-start(bf16[32,4,576]{2,1,0:T(4,128)(2,1)} %param.13) | copy-start | bytes 442372
  167.5 116.2 %all-to-all-start.2 = ((f32[1,32,128,512]{3,1,0,2:T(8,128)}), f32[1,32,128,512]{3,1,0,2:T(8,128)}, u32[]{:S(2)}, u32[]{:S(2)}) async-start(f32[1,32,128,512]{3,1,0,2:T(8,128)} %copy.90), calls=%async_computation.2 | async-start | bytes 16777216 | tf_op jit(solution)/shard_map/all_to_all | solution.py:84
  175.2 236.9 %all-reduce.3.cloned.1.call-start = ((), (), s32[]{:S(2)}) async-start(), calls=%async_computation.6 | async-start | bytes 917504
  288.5 5.4 copy-start.9
  288.5 123.6 %copy-start.4 = (bf16[1,7168]{1,0:T(2,128)(2,1)S(1)}, bf16[1,7168]{1,0:T(2,128)(2,1)}, u32[]{:S(2)}) copy-start(bf16[1,7168]{1,0:T(2,128)(2,1)} %param.19) | copy-start | bytes 43012
  288.5 127.1 %copy-start.5 = (f32[7168]{0:T(1024)S(1)}, f32[7168]{0:T(1024)}, u32[]{:S(2)}) copy-start(f32[7168]{0:T(1024)} %param.20) | copy-start | bytes 86020
  288.5 127.2 %copy-start.8 = (bf16[7168,16]{0,1:T(8,128)(2,1)S(1)}, bf16[7168,16]{0,1:T(8,128)(2,1)}, u32[]{:S(2)}) copy-start(bf16[7168,16]{0,1:T(8,128)(2,1)} %param.21) | copy-start | bytes 688132
  288.6 127.4 %copy-start.6 = (s32[1,8]{1,0:T(1,128)S(1)}, s32[1,8]{1,0:T(1,128)}, u32[]{:S(2)}) copy-start(s32[1,8]{1,0:T(1,128)} %param.22) | copy-start | bytes 100
Sparse Core Ops, SparseCore 0:
  294.0 118.0 all-reduce.2
